TPU v7x, 128 devices: a whole 4x4x4 slice. The times are simulated.
128 devices in a mesh: row: 8 (over y_lo, z), col: 16 (over x, y_hi, core).
Axes of the slice: x: 4, y: 4 (y_hi: 2, y_lo: 2; y = y_hi * 2 + y_lo), z: 4, core: 2. Of those that a mesh axis runs over, the one named last changes fastest.
Arguments:
- feats_one: bfloat16 [65536, 256], P(('row', 'col')), may hold values from -6 to 6
- feats_two: bfloat16 [65536, 256], P(('row', 'col')), may hold values from -6 to 6
- target_view: bfloat16 [65536, 256], P(('row', 'col')), may hold values from -6 to 6
- negatives: int32 [65536], P(('row', 'col')), may hold values from 0 to 511
- weight_one: bfloat16 [256, 256], replicated, may hold values from -0.375 to 0.375
- weight_two: bfloat16 [256, 256], replicated, may hold values from -0.375 to 0.375
- block_tiles: bfloat16 [81920, 128, 128], P(('row', 'col')), may hold values from -0.15625 to 0.15625
- tile_rows: int32 [81920], P(('row', 'col')), may hold values from 0 to 31
- tile_cols: int32 [81920], P(('row', 'col')), may hold values from 0 to 31
- block_counts: int32 [128], P(('row', 'col')), may hold values from 80 to 640, as said below
- need_rows: int32 [128, 16, 2], P(('row', 'col')), may hold values from 0 to 3, as said below
Outputs:
- grad_hidden: bfloat16 [65536, 256], P(('row', 'col'))
- grad_first: float32 [256, 256], replicated
- grad_second: float32 [256, 256], replicated
Inputs may be any that keep to these rules, and one draw needn't show every extreme that they name: `need_rows`: for each owner and source, the 2 entries are distinct. `block_counts`: live tiles of one block list.
All inputs are finite; a program needn't handle non-finite values.
Results may differ from a plain program's by a relative error of at most 0.0063.
Values may be sent and summed in bfloat16 or wider, within the bound.
No kernel may reach another device: no remote copies, remote signals or barrier semaphores. Data moves between devices by JAX's collectives and lax.ppermute only.
A program may use at most 192 MiB of HBM per device.

v0:
```python
import math
import jax
import jax.numpy as jnp
from jax import lax
from jax.sharding import PartitionSpec as P


def silu_slope(values):
    sig = jax.nn.sigmoid(values)
    return sig * (1.0 + values * (1.0 - sig))


def column_product(left, right):
    return lax.dot_general(
        left, right, (((0,), (0,)), ((), ())), preferred_element_type=jnp.float32
    )


def on_device(
    feats_one,
    feats_two,
    target_view,
    negatives,
    weight_one,
    weight_two,
    block_tiles,
    tile_rows,
    tile_cols,
    block_counts,
    need_rows,
):
    node_dev, features = feats_two.shape
    capacity, tile_size = (block_tiles.shape[0], block_tiles.shape[1])
    sources = lax.axis_size("col")
    row_group = lax.axis_size("row")
    tiles_dev = node_dev // tile_size
    slot_count = need_rows.shape[2]
    col_count = row_group * tiles_dev
    inverse_root = 1.0 / math.sqrt(features)
    weight_norm = 1.0 / math.sqrt(node_dev * row_group * sources)
    pre_two = jnp.dot(feats_two, weight_two, preferred_element_type=jnp.float32)
    hidden = jax.nn.silu(pre_two)
    partner_rows = hidden[negatives]
    target_full = target_view.astype(jnp.float32)
    s_pos = jnp.sum(hidden * target_full, axis=-1) * inverse_root
    s_neg = jnp.sum(hidden * partner_rows, axis=-1) * inverse_root
    prob_pos = jax.nn.sigmoid(-s_pos)
    prob_neg = jax.nn.sigmoid(s_neg)
    grad_out = -prob_pos[:, None] * target_full + prob_neg[:, None] * partner_rows
    grad_out = grad_out + jax.ops.segment_sum(
        prob_neg[:, None] * hidden, negatives, num_segments=node_dev
    )
    dpre_two = (grad_out * silu_slope(pre_two)).astype(jnp.bfloat16)
    grad_second = column_product(feats_two, dpre_two)
    grad_second = lax.psum(grad_second, ("row", "col"))
    message = lax.dot_general(
        dpre_two, weight_two, (((1,), (1,)), ((), ())), preferred_element_type=jnp.float32
    ).astype(jnp.bfloat16)
    gathered = lax.all_gather(message, "col", axis=0, tiled=True)
    buffer_tiles = gathered.reshape(sources * tiles_dev, tile_size, features)
    need_flat = need_rows[0].reshape(-1)
    slot_ids = jnp.arange(sources * slot_count, dtype=jnp.int32)
    local_tile = jnp.sum(
        jnp.where(tile_rows[:, None] == slot_ids[None, :], need_flat[None, :], 0), axis=1
    )
    row_tile = tile_rows // slot_count * tiles_dev + local_tile
    block_len = 128
    rounds = capacity // block_len
    live = (jnp.arange(capacity, dtype=jnp.int32) < block_counts[0]).astype(jnp.float32)
    column_ids = jnp.arange(col_count, dtype=jnp.int32)

    def add_block(summed_tiles, pieces):
        tile_part, row_part, col_part, live_part = pieces
        gathered_rows = buffer_tiles[row_part]
        contrib = jnp.einsum(
            "ktu,ktf->kuf", tile_part, gathered_rows, preferred_element_type=jnp.float32
        )
        selector = jnp.where(col_part[:, None] == column_ids[None, :], live_part[:, None], 0.0)
        placed = jnp.einsum(
            "kc,kuf->cuf",
            selector,
            contrib,
            precision=lax.Precision.HIGHEST,
            preferred_element_type=jnp.float32,
        )
        return (summed_tiles + placed, None)

    start_tiles = jnp.zeros((col_count, tile_size, features), jnp.float32)
    summed_tiles, _ = lax.scan(
        add_block,
        start_tiles,
        (
            block_tiles.reshape(rounds, block_len, tile_size, tile_size),
            row_tile.reshape(rounds, block_len),
            tile_cols.reshape(rounds, block_len),
            live.reshape(rounds, block_len),
        ),
    )
    column_total = lax.psum_scatter(
        summed_tiles.reshape(col_count * tile_size, features),
        "row",
        scatter_dimension=0,
        tiled=True,
    )
    grad_hidden = column_total.astype(jnp.bfloat16)
    pre_one = jnp.dot(feats_one, weight_one, preferred_element_type=jnp.float32)
    dpre_one = (grad_hidden.astype(jnp.float32) * silu_slope(pre_one)).astype(jnp.bfloat16)
    grad_first = column_product(feats_one, dpre_one)
    grad_first = lax.psum(grad_first, ("row", "col"))
    return (grad_hidden, grad_first * weight_norm, grad_second * weight_norm)


def solution(mesh):
    return jax.shard_map(
        on_device,
        mesh=mesh,
        in_specs=(
            P(("row", "col"), None),
            P(("row", "col"), None),
            P(("row", "col"), None),
            P(("row", "col")),
            P(),
            P(),
            P(("row", "col"), None, None),
            P(("row", "col")),
            P(("row", "col")),
            P(("row", "col")),
            P(("row", "col"), None, None),
        ),
        out_specs=(P(("row", "col"), None), P(), P()),
        check_vma=False,
    )
```

profile of v0, /device:TPU:1, one launch (start us, length us, event | category | flops | bytes accessed | tf_op | source)
XLA Modules:
  0.0 544.5 jit_solution(12721467284938459450)
XLA Ops:
  10.4 1.6 gather_fusion.1
  13.1 3.5 scatter_fusion
  18.1 27.9 %copy.40 = bf16[640,128,128]{1,2,0:T(8,128)(2,1)} copy(bf16[640,128,128]{2,1,0:T(8,128)(2,1)} %param.19) | data formatting | bytes 41943040 | tf_op args[6]
  47.0 30.8 %all-gather.2.cloned.1.call-done = bf16[8192,256]{1,0:T(8,128)(2,1)} async-done(((bf16[512,256]{1,0:T(8,128)(2,1)}), bf16[8192,256]{1,0:T(8,128)(2,1)}) %all-gather.2.cloned.1.call-update) | async-done | bytes 4194320 | tf_op jit(solution)/shard_map/all_gather | solution.py:59
  77.8 241.0 %while.11 = (s32[]{:T(128)}, f32[32,128,256]{2,0,1:T(8,128)}, s32[5,128]{1,0:T(8,128)}, f32[5,128]{1,0:T(8,128)S(1)}, bf16[5,128,128,128]{2,3,1,0:T(8,128)(2,1)}...) while((s32[]{:T(128)}, f32[32,128,256]{2,0,1:T(8,128)}, ...), condition=%wide.region_5.6_spmd.clone, body=%wide.region_4.5_spmd.clone.sunk | while | flops 2686461440 | bytes 71313008 | solution.py:89
  77.8 8.7 %gather_fusion = bf16[128,128,256]{2,1,0:T(8,128)(2,1)} fusion(bf16[64,128,256]{2,1,0:T(8,128)(2,1)} %get-tuple-element.172, s32[1024]{0:T(1024)S(1)} %pad_clamp_fusion.3), kind=kCustom, calls=%fused_computation.clone.clone.1 | custom fusion | bytes 16777728 | tf_op jit(solution)/shard_map/while/body/eval_jaxpr/gather | solution.py:74
  86.5 12.8 %fusion.55 = f32[128,128,256]{2,1,0:T(8,128)} fusion(bf16[128,128,256]{2,1,0:T(8,128)(2,1)} %gather_fusion, bf16[5,128,128,128]{2,3,1,0:T(8,128)(2,1)} %get-tuple-element.170, s32[]{:T(128)} %get-tuple-element.157), kind=kOutput, calls=%fused_computation.6.clone.1 | convolution fusion | flops 1073741824 | bytes 29360640 | tf_op jit(solution)/shard_map/while/body/eval_jaxpr/ktu,ktf->kuf/dot_general | solution.py:75
  100.0 25.4 %select_add_fusion.2 = f32[32,128,256]{2,0,1:T(8,128)} fusion(f32[32,128,256]{2,0,1:T(8,128)} %get-tuple-element.158, pred[]{:T(512)S(6)} %compare.5, f32[128,128,256]{2,1,0:T(8,128)} %fusion.55, f32[128]{0:T(128)S(1)} %fusion.56, s32[128]{0:T(128)S(1)} %fusion.57), kind=kOutput, calls=%fused_computation.8.clone.1 | convolution fusion | flops 1612718080 | bytes 25166848 | tf_op jit(solution)/shard_map/while/body/eval_jaxpr/kc,kuf->cuf/dot_general | solution.py:79
  125.5 8.7 %gather_fusion = bf16[128,128,256]{2,1,0:T(8,128)(2,1)} fusion(bf16[64,128,256]{2,1,0:T(8,128)(2,1)} %get-tuple-element.172, s32[1024]{0:T(1024)S(1)} %pad_clamp_fusion.3), kind=kCustom, calls=%fused_computation.clone.clone.1 | custom fusion | bytes 16777728 | tf_op jit(solution)/shard_map/while/body/eval_jaxpr/gather | solution.py:74
  134.2 12.8 %fusion.55 = f32[128,128,256]{2,1,0:T(8,128)} fusion(bf16[128,128,256]{2,1,0:T(8,128)(2,1)} %gather_fusion, bf16[5,128,128,128]{2,3,1,0:T(8,128)(2,1)} %get-tuple-element.170, s32[]{:T(128)} %get-tuple-element.157), kind=kOutput, calls=%fused_computation.6.clone.1 | convolution fusion | flops 1073741824 | bytes 29360640 | tf_op jit(solution)/shard_map/while/body/eval_jaxpr/ktu,ktf->kuf/dot_general | solution.py:75
  147.8 26.0 %select_add_fusion.2 = f32[32,128,256]{2,0,1:T(8,128)} fusion(f32[32,128,256]{2,0,1:T(8,128)} %get-tuple-element.158, pred[]{:T(512)S(6)} %compare.5, f32[128,128,256]{2,1,0:T(8,128)} %fusion.55, f32[128]{0:T(128)S(1)} %fusion.56, s32[128]{0:T(128)S(1)} %fusion.57), kind=kOutput, calls=%fused_computation.8.clone.1 | convolution fusion | flops 1612718080 | bytes 25166848 | tf_op jit(solution)/shard_map/while/body/eval_jaxpr/kc,kuf->cuf/dot_general | solution.py:79
  173.8 8.7 %gather_fusion = bf16[128,128,256]{2,1,0:T(8,128)(2,1)} fusion(bf16[64,128,256]{2,1,0:T(8,128)(2,1)} %get-tuple-element.172, s32[1024]{0:T(1024)S(1)} %pad_clamp_fusion.3), kind=kCustom, calls=%fused_computation.clone.clone.1 | custom fusion | bytes 16777728 | tf_op jit(solution)/shard_map/while/body/eval_jaxpr/gather | solution.py:74
  182.6 12.8 %fusion.55 = f32[128,128,256]{2,1,0:T(8,128)} fusion(bf16[128,128,256]{2,1,0:T(8,128)(2,1)} %gather_fusion, bf16[5,128,128,128]{2,3,1,0:T(8,128)(2,1)} %get-tuple-element.170, s32[]{:T(128)} %get-tuple-element.157), kind=kOutput, calls=%fused_computation.6.clone.1 | convolution fusion | flops 1073741824 | bytes 29360640 | tf_op jit(solution)/shard_map/while/body/eval_jaxpr/ktu,ktf->kuf/dot_general | solution.py:75
  196.1 26.0 %select_add_fusion.2 = f32[32,128,256]{2,0,1:T(8,128)} fusion(f32[32,128,256]{2,0,1:T(8,128)} %get-tuple-element.158, pred[]{:T(512)S(6)} %compare.5, f32[128,128,256]{2,1,0:T(8,128)} %fusion.55, f32[128]{0:T(128)S(1)} %fusion.56, s32[128]{0:T(128)S(1)} %fusion.57), kind=kOutput, calls=%fused_computation.8.clone.1 | convolution fusion | flops 1612718080 | bytes 25166848 | tf_op jit(solution)/shard_map/while/body/eval_jaxpr/kc,kuf->cuf/dot_general | solution.py:79
  222.2 8.8 %gather_fusion = bf16[128,128,256]{2,1,0:T(8,128)(2,1)} fusion(bf16[64,128,256]{2,1,0:T(8,128)(2,1)} %get-tuple-element.172, s32[1024]{0:T(1024)S(1)} %pad_clamp_fusion.3), kind=kCustom, calls=%fused_computation.clone.clone.1 | custom fusion | bytes 16777728 | tf_op jit(solution)/shard_map/while/body/eval_jaxpr/gather | solution.py:74
  230.9 12.8 %fusion.55 = f32[128,128,256]{2,1,0:T(8,128)} fusion(bf16[128,128,256]{2,1,0:T(8,128)(2,1)} %gather_fusion, bf16[5,128,128,128]{2,3,1,0:T(8,128)(2,1)} %get-tuple-element.170, s32[]{:T(128)} %get-tuple-element.157), kind=kOutput, calls=%fused_computation.6.clone.1 | convolution fusion | flops 1073741824 | bytes 29360640 | tf_op jit(solution)/shard_map/while/body/eval_jaxpr/ktu,ktf->kuf/dot_general | solution.py:75
  244.4 26.0 %select_add_fusion.2 = f32[32,128,256]{2,0,1:T(8,128)} fusion(f32[32,128,256]{2,0,1:T(8,128)} %get-tuple-element.158, pred[]{:T(512)S(6)} %compare.5, f32[128,128,256]{2,1,0:T(8,128)} %fusion.55, f32[128]{0:T(128)S(1)} %fusion.56, s32[128]{0:T(128)S(1)} %fusion.57), kind=kOutput, calls=%fused_computation.8.clone.1 | convolution fusion | flops 1612718080 | bytes 25166848 | tf_op jit(solution)/shard_map/while/body/eval_jaxpr/kc,kuf->cuf/dot_general | solution.py:79
  270.5 8.7 %gather_fusion = bf16[128,128,256]{2,1,0:T(8,128)(2,1)} fusion(bf16[64,128,256]{2,1,0:T(8,128)(2,1)} %get-tuple-element.172, s32[1024]{0:T(1024)S(1)} %pad_clamp_fusion.3), kind=kCustom, calls=%fused_computation.clone.clone.1 | custom fusion | bytes 16777728 | tf_op jit(solution)/shard_map/while/body/eval_jaxpr/gather | solution.py:74
  279.2 12.8 %fusion.55 = f32[128,128,256]{2,1,0:T(8,128)} fusion(bf16[128,128,256]{2,1,0:T(8,128)(2,1)} %gather_fusion, bf16[5,128,128,128]{2,3,1,0:T(8,128)(2,1)} %get-tuple-element.170, s32[]{:T(128)} %get-tuple-element.157), kind=kOutput, calls=%fused_computation.6.clone.1 | convolution fusion | flops 1073741824 | bytes 29360640 | tf_op jit(solution)/shard_map/while/body/eval_jaxpr/ktu,ktf->kuf/dot_general | solution.py:75
  292.8 26.0 %select_add_fusion.2 = f32[32,128,256]{2,0,1:T(8,128)} fusion(f32[32,128,256]{2,0,1:T(8,128)} %get-tuple-element.158, pred[]{:T(512)S(6)} %compare.5, f32[128,128,256]{2,1,0:T(8,128)} %fusion.55, f32[128]{0:T(128)S(1)} %fusion.56, s32[128]{0:T(128)S(1)} %fusion.57), kind=kOutput, calls=%fused_computation.8.clone.1 | convolution fusion | flops 1612718080 | bytes 25166848 | tf_op jit(solution)/shard_map/while/body/eval_jaxpr/kc,kuf->cuf/dot_general | solution.py:79
  318.8 5.9 %copy.49 = f32[32,128,256]{1,0,2:T(8,128)} copy(f32[32,128,256]{2,0,1:T(8,128)} %get-tuple-element.45) | data formatting | bytes 8388608 | tf_op jit(solution)/shard_map/while | solution.py:89
  324.8 8.0 %copy.62 = f32[32,8,32,128]{3,1,2,0:T(8,128)} copy(f32[32,8,32,128]{3,2,1,0:T(8,128)} %bitcast.62) | data formatting | bytes 8388608
  333.8 50.9 %reduce-scatter.2.cloned.1.call-done = f32[512,256]{0,1:T(8,128)} async-done(((f32[4096,256]{0,1:T(8,128)}), f32[512,256]{0,1:T(8,128)}) %reduce-scatter.2.cloned.1.call-update) | async-done | bytes 524304 | tf_op jit(solution)/shard_map/reduce_scatter | solution.py:99
  387.9 146.5 %all-reduce.3.cloned.1.call-done = (f32[256,256]{0,1:T(8,128)}, f32[256,256]{0,1:T(8,128)}) async-done(((f32[256,256]{0,1:T(8,128)}, f32[256,256]{0,1:T(8,128)}), (f32[256,256]{0,1:T(8,128)}, f32[256,256]{0,1:T(8,128)})) %all-reduce.3.cloned.1.call-update) | async-done | bytes 524304 | tf_op jit(solution)/shard_map/psum | solution.py:109
  (70 shorter events, 17.2 us)
Async XLA Ops:
  7.2 1.0 copy-start
  7.2 5.9 %copy-start.4 = (s32[512]{0:T(512)S(1)}, s32[512]{0:T(512)}, u32[]{:S(2)}) copy-start(s32[512]{0:T(512)} %param.16) | copy-start | bytes 6148
  7.2 4.9 copy-start.1
  7.2 70.6 %all-gather.2.cloned.1.call-start = ((), (), s32[]{:S(2)}) async-start(), calls=%async_computation.1 | async-start | bytes 4456448 | tf_op jit(solution)/shard_map/all_gather | solution.py:59
  12.3 4.7 copy-start.2
  18.0 366.7 %reduce-scatter.2.cloned.1.call-start = ((), (), s32[]{:S(2)}) async-start(), calls=%async_computation.2 | async-start | bytes 4718592 | tf_op jit(solution)/shard_map/reduce_scatter | solution.py:99
  18.1 27.9 %copy-start.5 = (s32[1,16,2]{1,2,0:T(2,128)S(1)}, s32[1,16,2]{1,2,0:T(2,128)}, u32[]{:S(2)}) copy-start(s32[1,16,2]{1,2,0:T(2,128)} %param.23) | copy-start | bytes 388
  18.1 28.8 %copy-start.3 = (s32[640]{0:T(1024)S(1)}, s32[640]{0:T(1024)}, u32[]{:S(2)}) copy-start(s32[640]{0:T(1024)} %param.20) | copy-start | bytes 7684
  324.8 61.0 %copy-start.6 = (bf16[512,256]{1,0:T(8,128)(2,1)S(1)}, bf16[512,256]{1,0:T(8,128)(2,1)}, u32[]{:S(2)}) copy-start(bf16[512,256]{1,0:T(8,128)(2,1)} %param.13) | copy-start | bytes 786436
  324.8 61.0 %copy-start.7 = (bf16[256,256]{1,0:T(8,128)(2,1)S(1)}, bf16[256,256]{1,0:T(8,128)(2,1)}, u32[]{:S(2)}) copy-start(bf16[256,256]{1,0:T(8,128)(2,1)} %param.17) | copy-start | bytes 393220
  332.8 201.6 %all-reduce.3.cloned.1.call-start = ((), (), s32[]{:S(2)}) async-start(), calls=%async_computation.3 | async-start | bytes 1048576 | tf_op jit(solution)/shard_map/psum | solution.py:109
Sparse Core Ops, SparseCore 0:
  18.2 59.5 all-gather.1
  332.9 51.7 reduce-scatter.1
  390.2 144.0 all-reduce.2
where the time goes:
time: 546 us; the launch traced here: 544 us
  waiting for transfers between devices  228 us (42%)
  matrix products  198 us (36%)
  local copies, waits for them, and re-layouts  95.4 us (17%)
  between operations  14.6 us (3%)
  other arithmetic  7.94 us (1%)
    psum x1, waiting for transfers between devices, on_device(): grad_first = lax.psum(grad_first, ('row', 'col'))  146 us
    dot_general x5, matrix products, add_block(): jnp.einsum('kc,kuf->cuf', selector, contrib, precision=lax.Precision.HIGH...  130 us
    dot_general x5, matrix products, add_block(): jnp.einsum('ktu,ktf->kuf', tile_part, gathered_rows, preferred_element_ty...  64.1 us
    reduce_scatter x1, waiting for transfers between devices, on_device(): lax.psum_scatter(summed_tiles.reshape(col_count * tile_size, features), '...  50.9 us
    gather x5, local copies, waits for them, and re-layouts, add_block(): gathered_rows = buffer_tiles[row_part]  43.7 us
    unnamed x23, local copies, waits for them, and re-layouts  39.7 us
    all_gather x1, waiting for transfers between devices, on_device(): gathered = lax.all_gather(message, 'col', axis=0, tiled=True)  30.8 us
  transfers between devices with their start and end apart: 3, of which 3 were waited for; matrix products, arithmetic and copies ran while one was open for 6% of the time, Pallas kernels for 0%

commit v1 on v0

--- a/solution.py
+++ b/solution.py
@@ -3,6 +3,12 @@
 import jax.numpy as jnp
 from jax import lax
 from jax.sharding import PartitionSpec as P
+
+
+def summed_here(array, mesh_axis):
+    parts = lax.all_gather(array, mesh_axis, axis=0, tiled=False)
+    summed = parts.sum(axis=0)
+    return summed
 
 
 def silu_slope(values):
@@ -106,7 +112,7 @@
     pre_one = jnp.dot(feats_one, weight_one, preferred_element_type=jnp.float32)
     dpre_one = (grad_hidden.astype(jnp.float32) * silu_slope(pre_one)).astype(jnp.bfloat16)
     grad_first = column_product(feats_one, dpre_one)
-    grad_first = lax.psum(grad_first, ("row", "col"))
+    grad_first = summed_here(grad_first, ("row", "col"))
     return (grad_hidden, grad_first * weight_norm, grad_second * weight_norm)
 
 

time: 546 us -> 766 us (1.40)
  waiting for transfers between devices: 228 us -> 425 us
  local copies, waits for them, and re-layouts: 95.4 us -> 125 us
  matrix products: 198 us -> 186 us
    all_gather x0 -> x1, waiting for transfers between devices: none -> 235 us  [summed_here(): parts = lax.all_gather(array, mesh_axis, axis=0, tiled=False)]
    psum x1, waiting for transfers between devices: 146 us -> 108 us  [on_device(): grad_second = lax.psum(grad_second, ('row', 'col'))]
    unnamed x23 -> x22, local copies, waits for them, and re-layouts: 39.7 us -> 59.2 us
    dot_general x5, matrix products: 130 us -> 117 us  [add_block(): jnp.einsum('kc,kuf->cuf', selector, contrib, precision=lax.Precision.HIGH...]
    while x0 -> x20, local copies, waits for them, and re-layouts: none -> 10.2 us
  transfers between devices with their start and end apart: 3 -> 4, of which waited for: 3 -> 4; matrix products, arithmetic and copies ran while one was open for 6% -> 4% of each run, Pallas kernels for 0% -> 0%
where the time goes in v1:
time: 766 us; the launch traced here: 765 us
  waiting for transfers between devices  425 us (55%)
  matrix products  186 us (24%)
  local copies, waits for them, and re-layouts  125 us (16%)
  between operations  16.4 us (2%)
  other arithmetic  11.1 us (1%)
    all_gather x1, waiting for transfers between devices, summed_here(): parts = lax.all_gather(array, mesh_axis, axis=0, tiled=False)  235 us
    dot_general x5, matrix products, add_block(): jnp.einsum('kc,kuf->cuf', selector, contrib, precision=lax.Precision.HIGH...  117 us
    psum x1, waiting for transfers between devices, on_device(): grad_second = lax.psum(grad_second, ('row', 'col'))  108 us
    dot_general x5, matrix products, add_block(): jnp.einsum('ktu,ktf->kuf', tile_part, gathered_rows, preferred_element_ty...  64.8 us
    unnamed x22, local copies, waits for them, and re-layouts  59.2 us
    reduce_scatter x1, waiting for transfers between devices, on_device(): lax.psum_scatter(summed_tiles.reshape(col_count * tile_size, features), '...  50.9 us
    gather x5, local copies, waits for them, and re-layouts, add_block(): gathered_rows = buffer_tiles[row_part]  43.7 us
    all_gather x1, waiting for transfers between devices, on_device(): gathered = lax.all_gather(message, 'col', axis=0, tiled=True)  30.7 us
  transfers between devices with their start and end apart: 4, of which 4 were waited for; matrix products, arithmetic and copies ran while one was open for 4% of the time, Pallas kernels for 0%

profile of v1, /device:TPU:1, one launch (start us, length us, event | category | flops | bytes accessed | tf_op | source)
XLA Modules:
  0.0 764.6 jit_solution(1704725487157319184)
XLA Ops:
  20.0 27.9 %copy.40 = bf16[640,128,128]{1,2,0:T(8,128)(2,1)} copy(bf16[640,128,128]{2,1,0:T(8,128)(2,1)} %param.19) | data formatting | bytes 41943040 | tf_op args[6]
  48.0 30.7 %all-gather.4.cloned.1.call-done = bf16[8192,256]{1,0:T(8,128)(2,1)} async-done(((bf16[512,256]{1,0:T(8,128)(2,1)}), bf16[8192,256]{1,0:T(8,128)(2,1)}) %all-gather.4.cloned.1.call-update) | async-done | bytes 4194320 | tf_op jit(solution)/shard_map/all_gather | solution.py:65
  78.7 239.5 %while.11 = (s32[]{:T(128)}, f32[32,128,256]{2,0,1:T(8,128)}, s32[5,128]{1,0:T(8,128)}, f32[5,128]{1,0:T(8,128)S(1)}, bf16[5,128,128,128]{2,3,1,0:T(8,128)(2,1)}...) while((s32[]{:T(128)}, f32[32,128,256]{2,0,1:T(8,128)}, ...), condition=%wide.region_5.6_spmd.clone, body=%wide.region_4.5_spmd.clone.sunk | while | flops 2686461440 | bytes 104867000 | solution.py:95
  79.4 8.7 %gather_fusion = bf16[128,128,256]{2,1,0:T(8,128)(2,1)} fusion(bf16[64,128,256]{2,1,0:T(8,128)(2,1)} %get-tuple-element.170, s32[1024]{0:T(1024)S(1)} %pad_clamp_fusion.3), kind=kCustom, calls=%fused_computation.clone.clone.1 | custom fusion | bytes 16777728 | tf_op jit(solution)/shard_map/while/body/eval_jaxpr/gather | solution.py:80
  88.1 13.0 %fusion.55 = f32[128,128,256]{2,1,0:T(8,128)} fusion(bf16[128,128,256]{2,1,0:T(8,128)(2,1)} %gather_fusion, bf16[5,128,128,128]{2,3,1,0:T(8,128)(2,1)} %get-tuple-element.168, s32[]{:T(128)S(6)} %copy.69), kind=kOutput, calls=%fused_computation.6.clone.1 | convolution fusion | flops 1073741824 | bytes 29360132 | tf_op jit(solution)/shard_map/while/body/eval_jaxpr/ktu,ktf->kuf/dot_general | solution.py:81
  101.1 23.4 %select_add_fusion.2 = f32[32,128,256]{2,0,1:T(8,128)S(1)} fusion(f32[32,128,256]{2,0,1:T(8,128)S(1)} %copy-done.1, pred[]{:T(512)S(6)} %compare.5, f32[128,128,256]{2,1,0:T(8,128)} %fusion.55, f32[128]{0:T(128)S(1)} %fusion.56, s32[128]{0:T(128)S(1)} %fusion.57), kind=kOutput, calls=%fused_computation.8.clone.1 | convolution fusion | flops 1612718080 | bytes 25166848 | tf_op jit(solution)/shard_map/while/body/eval_jaxpr/kc,kuf->cuf/dot_general | solution.py:85
  127.3 8.7 %gather_fusion = bf16[128,128,256]{2,1,0:T(8,128)(2,1)} fusion(bf16[64,128,256]{2,1,0:T(8,128)(2,1)} %get-tuple-element.170, s32[1024]{0:T(1024)S(1)} %pad_clamp_fusion.3), kind=kCustom, calls=%fused_computation.clone.clone.1 | custom fusion | bytes 16777728 | tf_op jit(solution)/shard_map/while/body/eval_jaxpr/gather | solution.py:80
  136.0 13.0 %fusion.55 = f32[128,128,256]{2,1,0:T(8,128)} fusion(bf16[128,128,256]{2,1,0:T(8,128)(2,1)} %gather_fusion, bf16[5,128,128,128]{2,3,1,0:T(8,128)(2,1)} %get-tuple-element.168, s32[]{:T(128)S(6)} %copy.69), kind=kOutput, calls=%fused_computation.6.clone.1 | convolution fusion | flops 1073741824 | bytes 29360132 | tf_op jit(solution)/shard_map/while/body/eval_jaxpr/ktu,ktf->kuf/dot_general | solution.py:81
  149.0 23.4 %select_add_fusion.2 = f32[32,128,256]{2,0,1:T(8,128)S(1)} fusion(f32[32,128,256]{2,0,1:T(8,128)S(1)} %copy-done.1, pred[]{:T(512)S(6)} %compare.5, f32[128,128,256]{2,1,0:T(8,128)} %fusion.55, f32[128]{0:T(128)S(1)} %fusion.56, s32[128]{0:T(128)S(1)} %fusion.57), kind=kOutput, calls=%fused_computation.8.clone.1 | convolution fusion | flops 1612718080 | bytes 25166848 | tf_op jit(solution)/shard_map/while/body/eval_jaxpr/kc,kuf->cuf/dot_general | solution.py:85
  175.2 8.7 %gather_fusion = bf16[128,128,256]{2,1,0:T(8,128)(2,1)} fusion(bf16[64,128,256]{2,1,0:T(8,128)(2,1)} %get-tuple-element.170, s32[1024]{0:T(1024)S(1)} %pad_clamp_fusion.3), kind=kCustom, calls=%fused_computation.clone.clone.1 | custom fusion | bytes 16777728 | tf_op jit(solution)/shard_map/while/body/eval_jaxpr/gather | solution.py:80
  183.9 13.0 %fusion.55 = f32[128,128,256]{2,1,0:T(8,128)} fusion(bf16[128,128,256]{2,1,0:T(8,128)(2,1)} %gather_fusion, bf16[5,128,128,128]{2,3,1,0:T(8,128)(2,1)} %get-tuple-element.168, s32[]{:T(128)S(6)} %copy.69), kind=kOutput, calls=%fused_computation.6.clone.1 | convolution fusion | flops 1073741824 | bytes 29360132 | tf_op jit(solution)/shard_map/while/body/eval_jaxpr/ktu,ktf->kuf/dot_general | solution.py:81
  196.9 23.4 %select_add_fusion.2 = f32[32,128,256]{2,0,1:T(8,128)S(1)} fusion(f32[32,128,256]{2,0,1:T(8,128)S(1)} %copy-done.1, pred[]{:T(512)S(6)} %compare.5, f32[128,128,256]{2,1,0:T(8,128)} %fusion.55, f32[128]{0:T(128)S(1)} %fusion.56, s32[128]{0:T(128)S(1)} %fusion.57), kind=kOutput, calls=%fused_computation.8.clone.1 | convolution fusion | flops 1612718080 | bytes 25166848 | tf_op jit(solution)/shard_map/while/body/eval_jaxpr/kc,kuf->cuf/dot_general | solution.py:85
  223.1 8.8 %gather_fusion = bf16[128,128,256]{2,1,0:T(8,128)(2,1)} fusion(bf16[64,128,256]{2,1,0:T(8,128)(2,1)} %get-tuple-element.170, s32[1024]{0:T(1024)S(1)} %pad_clamp_fusion.3), kind=kCustom, calls=%fused_computation.clone.clone.1 | custom fusion | bytes 16777728 | tf_op jit(solution)/shard_map/while/body/eval_jaxpr/gather | solution.py:80
  231.8 13.0 %fusion.55 = f32[128,128,256]{2,1,0:T(8,128)} fusion(bf16[128,128,256]{2,1,0:T(8,128)(2,1)} %gather_fusion, bf16[5,128,128,128]{2,3,1,0:T(8,128)(2,1)} %get-tuple-element.168, s32[]{:T(128)S(6)} %copy.69), kind=kOutput, calls=%fused_computation.6.clone.1 | convolution fusion | flops 1073741824 | bytes 29360132 | tf_op jit(solution)/shard_map/while/body/eval_jaxpr/ktu,ktf->kuf/dot_general | solution.py:81
  244.8 23.4 %select_add_fusion.2 = f32[32,128,256]{2,0,1:T(8,128)S(1)} fusion(f32[32,128,256]{2,0,1:T(8,128)S(1)} %copy-done.1, pred[]{:T(512)S(6)} %compare.5, f32[128,128,256]{2,1,0:T(8,128)} %fusion.55, f32[128]{0:T(128)S(1)} %fusion.56, s32[128]{0:T(128)S(1)} %fusion.57), kind=kOutput, calls=%fused_computation.8.clone.1 | convolution fusion | flops 1612718080 | bytes 25166848 | tf_op jit(solution)/shard_map/while/body/eval_jaxpr/kc,kuf->cuf/dot_general | solution.py:85
  271.0 8.8 %gather_fusion = bf16[128,128,256]{2,1,0:T(8,128)(2,1)} fusion(bf16[64,128,256]{2,1,0:T(8,128)(2,1)} %get-tuple-element.170, s32[1024]{0:T(1024)S(1)} %pad_clamp_fusion.3), kind=kCustom, calls=%fused_computation.clone.clone.1 | custom fusion | bytes 16777728 | tf_op jit(solution)/shard_map/while/body/eval_jaxpr/gather | solution.py:80
  279.7 13.0 %fusion.55 = f32[128,128,256]{2,1,0:T(8,128)} fusion(bf16[128,128,256]{2,1,0:T(8,128)(2,1)} %gather_fusion, bf16[5,128,128,128]{2,3,1,0:T(8,128)(2,1)} %get-tuple-element.168, s32[]{:T(128)S(6)} %copy.69), kind=kOutput, calls=%fused_computation.6.clone.1 | convolution fusion | flops 1073741824 | bytes 29360132 | tf_op jit(solution)/shard_map/while/body/eval_jaxpr/ktu,ktf->kuf/dot_general | solution.py:81
  292.7 23.4 %select_add_fusion.2 = f32[32,128,256]{2,0,1:T(8,128)S(1)} fusion(f32[32,128,256]{2,0,1:T(8,128)S(1)} %copy-done.1, pred[]{:T(512)S(6)} %compare.5, f32[128,128,256]{2,1,0:T(8,128)} %fusion.55, f32[128]{0:T(128)S(1)} %fusion.56, s32[128]{0:T(128)S(1)} %fusion.57), kind=kOutput, calls=%fused_computation.8.clone.1 | convolution fusion | flops 1612718080 | bytes 25166848 | tf_op jit(solution)/shard_map/while/body/eval_jaxpr/kc,kuf->cuf/dot_general | solution.py:85
  318.2 5.9 copy.49
  324.1 8.0 %copy.63 = f32[32,8,32,128]{3,1,2,0:T(8,128)} copy(f32[32,8,32,128]{3,2,1,0:T(8,128)} %bitcast.68) | data formatting | bytes 8388608
  333.2 50.9 %reduce-scatter.2.cloned.1.call-done = f32[512,256]{0,1:T(8,128)} async-done(((f32[4096,256]{0,1:T(8,128)}), f32[512,256]{0,1:T(8,128)}) %reduce-scatter.2.cloned.1.call-update) | async-done | bytes 524304 | tf_op jit(solution)/shard_map/reduce_scatter | solution.py:105
  386.4 108.4 %all-reduce.2.cloned.1.call-done = f32[256,256]{0,1:T(8,128)} async-done(((f32[256,256]{0,1:T(8,128)}), f32[256,256]{0,1:T(8,128)}) %all-reduce.2.cloned.1.call-update) | async-done | bytes 262160 | tf_op jit(solution)/shard_map/psum | solution.py:61
  497.4 235.2 %all-gather.6.cloned.1.call-done = f32[32768,256]{0,1:T(8,128)} async-done(((f32[256,256]{0,1:T(8,128)}), f32[32768,256]{0,1:T(8,128)}) %all-gather.6.cloned.1.call-update) | async-done | bytes 33554448 | tf_op jit(solution)/shard_map/all_gather | solution.py:9
  732.6 19.6 %copy.57 = f32[32,8,128,256]{3,2,1,0:T(8,128)S(1)} copy(f32[32,8,128,256]{3,1,2,0:T(8,128)} %bitcast.66) | data formatting | bytes 67108864
  (93 shorter events, 36.0 us)
Async XLA Ops:
  8.0 1.9 copy-start
  8.0 5.9 copy-start.5
  8.0 70.6 %all-gather.4.cloned.1.call-start = ((), (), s32[]{:S(2)}) async-start(), calls=%async_computation.1 | async-start | bytes 4456448 | tf_op jit(solution)/shard_map/all_gather | solution.py:65
  13.1 4.7 copy-start.3
  13.3 6.5 copy-start.6
  18.9 365.2 %reduce-scatter.2.cloned.1.call-start = ((), (), s32[]{:S(2)}) async-start(), calls=%async_computation.2 | async-start | bytes 4718592 | tf_op jit(solution)/shard_map/reduce_scatter | solution.py:105
  20.0 27.9 %copy-start.4 = (s32[640]{0:T(1024)S(1)}, s32[640]{0:T(1024)}, u32[]{:S(2)}) copy-start(s32[640]{0:T(1024)} %param.20) | copy-start | bytes 7684
  88.1 13.0 %copy-start.1 = (f32[32,128,256]{2,0,1:T(8,128)S(1)}, f32[32,128,256]{2,0,1:T(8,128)}, u32[]{:S(2)}) copy-start(f32[32,128,256]{2,0,1:T(8,128)} %get-tuple-element.156) | copy-start | bytes 12582916 | tf_op jit(solution)/shard_map/while
  124.5 2.0 copy-start.2
  136.0 13.0 %copy-start.1 = (f32[32,128,256]{2,0,1:T(8,128)S(1)}, f32[32,128,256]{2,0,1:T(8,128)}, u32[]{:S(2)}) copy-start(f32[32,128,256]{2,0,1:T(8,128)} %get-tuple-element.156) | copy-start | bytes 12582916 | tf_op jit(solution)/shard_map/while
  172.4 2.0 copy-start.2
  183.9 13.0 %copy-start.1 = (f32[32,128,256]{2,0,1:T(8,128)S(1)}, f32[32,128,256]{2,0,1:T(8,128)}, u32[]{:S(2)}) copy-start(f32[32,128,256]{2,0,1:T(8,128)} %get-tuple-element.156) | copy-start | bytes 12582916 | tf_op jit(solution)/shard_map/while
  220.3 2.0 copy-start.2
  231.8 13.0 %copy-start.1 = (f32[32,128,256]{2,0,1:T(8,128)S(1)}, f32[32,128,256]{2,0,1:T(8,128)}, u32[]{:S(2)}) copy-start(f32[32,128,256]{2,0,1:T(8,128)} %get-tuple-element.156) | copy-start | bytes 12582916 | tf_op jit(solution)/shard_map/while
  268.2 2.0 copy-start.2
  279.7 13.0 %copy-start.1 = (f32[32,128,256]{2,0,1:T(8,128)S(1)}, f32[32,128,256]{2,0,1:T(8,128)}, u32[]{:S(2)}) copy-start(f32[32,128,256]{2,0,1:T(8,128)} %get-tuple-element.156) | copy-start | bytes 12582916 | tf_op jit(solution)/shard_map/while
  316.1 2.0 copy-start.2
  324.1 61.0 %copy-start.7 = (bf16[512,256]{1,0:T(8,128)(2,1)S(1)}, bf16[512,256]{1,0:T(8,128)(2,1)}, u32[]{:S(2)}) copy-start(bf16[512,256]{1,0:T(8,128)(2,1)} %param.13) | copy-start | bytes 786436
  324.1 61.0 %copy-start.8 = (bf16[256,256]{1,0:T(8,128)(2,1)S(1)}, bf16[256,256]{1,0:T(8,128)(2,1)}, u32[]{:S(2)}) copy-start(bf16[256,256]{1,0:T(8,128)(2,1)} %param.17) | copy-start | bytes 393220
  332.1 162.7 %all-reduce.2.cloned.1.call-start = ((), (), s32[]{:S(2)}) async-start(), calls=%async_computation.3 | async-start | bytes 524288 | tf_op jit(solution)/shard_map/psum | solution.py:61
  333.1 399.5 %all-gather.6.cloned.1.call-start = ((), (), s32[]{:S(2)}) async-start(), calls=%async_computation.4 | async-start | bytes 33816576 | tf_op jit(solution)/shard_map/all_gather | solution.py:9
Sparse Core Ops, SparseCore 0:
  19.0 59.5 all-gather.3
  332.2 51.7 reduce-scatter.1
Sparse Core Ops, SparseCore 1:
  337.9 156.8 all-reduce.1
  497.0 235.6 all-gather.5
